TPU v7x, 32 devices: a whole 2x2x4 slice. The times are simulated.
32 devices in a mesh: groups: 2 (over y), space: 16 (over z, x, core).
Axes of the slice: x: 2, y: 2, z: 4, core: 2. Of those that a mesh axis runs over, the one named last changes fastest.
Arguments:
- modes: float32 [4, 128, 32, 64], P('groups', None, 'space'), parts along dimension 0, may hold values from -6 to 6
- cell_weight: float32 [32, 128], P('space', 'groups'), parts along dimension 1, may hold values from 0.5 to 2
- seeds: int32 [256], P(('groups', 'space')), parts along dimension 0, may hold values from 0 to 255
- coeff_table: float32 [256, 128], replicated, may hold values from -6 to 6
- force_table: float32 [256, 128], replicated, may hold values from -6 to 6
- visc_table: float32 [256], replicated, may hold values from 0.02 to 0.2
Outputs:
- coefficients: float32 [256, 128], P(('groups', 'space')), parts along dimension 0
There are 2 independent parts, one for each index of `groups`. A program takes and returns all parts, laid end to end along the dimension named above; an argument that names none is the same for every part. Nothing has to cross between parts.
All inputs are finite; a program needn't handle non-finite values.
Results may differ from a plain program's by a relative error of at most 0.00013.
Values sent between devices are 32-bit elements; how exact they have to be, the bound alone decides.
A program may use at most 64 MiB of HBM per device.

v0:
```python
import math
import jax
import jax.numpy as jnp
from jax import lax
from jax.sharding import PartitionSpec as P

STEPS = 2
TIME_STEP = 0.5


def padded_2(array, sides, width):
    for axis, dim in sides:
        devices, length = (lax.axis_size(axis), array.shape[dim])
        up = [(i, (i + 1) % devices) for i in range(devices)]
        down = [(j, i) for i, j in up]
        last = lax.slice_in_dim(array, length - width, length, axis=dim)
        first = lax.slice_in_dim(array, 0, width, axis=dim)
        before = lax.ppermute(last, axis, up)
        after = lax.ppermute(first, axis, down)
        array = jnp.concatenate([before, array, after], axis=dim)
    return array


def shards(modes, cell_weight, seeds, coeff_table, force_table, visc_table):
    mode_count = modes.shape[1]
    slab_cells = modes.shape[2]
    across = modes.shape[3]
    devices = lax.axis_size("space")
    cell_count = slab_cells * across
    total_cells = cell_count * devices
    padded = padded_2(modes, (("space", 2),), 2)
    slope_along = (
        padded[:, :, 0:slab_cells]
        - 8.0 * padded[:, :, 1 : slab_cells + 1]
        + 8.0 * padded[:, :, 3 : slab_cells + 3]
        - padded[:, :, 4 : slab_cells + 4]
    ) / 12.0
    slope_across = (
        jnp.roll(modes, 2, 3)
        - 8.0 * jnp.roll(modes, 1, 3)
        + 8.0 * jnp.roll(modes, -1, 3)
        - jnp.roll(modes, -2, 3)
    ) / 12.0
    slopes = jnp.stack([slope_along, slope_across]).reshape(2, 2, mode_count, cell_count)
    velocity = modes.reshape(2, mode_count, cell_count)
    cell_scale = cell_weight.reshape(cell_count) / total_cells
    weighted = velocity * cell_scale[None, None, :]
    diffusion = lax.psum(
        jnp.einsum(
            "taic,tajc->ij",
            slopes * cell_scale[None, None, None, :],
            slopes,
            precision=lax.Precision.HIGHEST,
        ),
        "space",
    )
    selector = (
        seeds[:, None] == jnp.arange(coeff_table.shape[0], dtype=jnp.int32)[None, :]
    ).astype(jnp.float32)
    coeffs = jnp.dot(selector, coeff_table, precision=lax.Precision.HIGHEST)
    forcing = jnp.dot(selector, force_table, precision=lax.Precision.HIGHEST)
    viscosity = jnp.dot(selector, visc_table, precision=lax.Precision.HIGHEST)
    own_count = coeffs.shape[0]

    def field_block(coeff_rows):
        flow = jnp.einsum("ni,aic->anc", coeff_rows, velocity, precision=lax.Precision.HIGHEST)
        grads = jnp.einsum("nk,takc->tanc", coeff_rows, slopes, precision=lax.Precision.HIGHEST)
        carried = jnp.sum(flow[:, None, :, :] * grads, axis=0)
        return jnp.einsum("aic,anc->ni", weighted, carried, precision=lax.Precision.HIGHEST)

    for repeat in range(STEPS):
        everyone = lax.all_gather(coeffs, "space", axis=0, tiled=True)
        rows_each = math.gcd(own_count * lax.axis_size("space"), 128)
        stacked = everyone.reshape(
            own_count * lax.axis_size("space") // rows_each, rows_each, mode_count
        )
        quadratic = lax.psum_scatter(
            lax.map(field_block, stacked).reshape(own_count * lax.axis_size("space"), mode_count),
            "space",
            scatter_dimension=0,
            tiled=True,
        )
        linear = jnp.dot(coeffs, diffusion, precision=lax.Precision.HIGHEST)
        coeffs = coeffs + TIME_STEP * (forcing - viscosity[:, None] * linear - quadratic)
    return coeffs


def solution(mesh):
    placed = (
        P("groups", None, "space", None),
        P("space", "groups"),
        P(("groups", "space")),
        P(),
        P(),
        P(),
    )
    return jax.shard_map(
        shards, mesh=mesh, in_specs=placed, out_specs=P(("groups", "space"), None), check_vma=False
    )
```

profile of v0, /device:TPU:8, one launch (start us, length us, event | category | flops | bytes accessed | tf_op | source)
XLA Modules:
  0.0 243.6 jit_solution(18027088971304564999)
XLA Ops:
  6.5 0.0 copy-start
  6.5 0.0 copy-start.1
  6.5 0.0 all-reduce.8.cloned.1.call-start
  6.5 0.0 collective-permute-start
  6.6 2.6 %collective-permute-start.1 = (f32[2,128,2,64]{1,3,2,0:T(8,128)}, f32[2,128,2,64]{1,3,2,0:T(8,128)S(1)}, u32[]{:S(2)}, u32[]{:S(2)}) collective-permute-start(f32[2,128,2,64]{1,3,2,0:T(8,128)} %param.6), channel_id=1, source_target_pairs={{1,0},{2,1},{3,2},{4,3},{5,4},{6,5},{7,6},{8,7},{9,8},{10,9},{11,1... | collective-permute-start | bytes 393224 | tf_op jit(solution)/shard_map/ppermute | solution.py:19
  9.2 1.0 slice_bitcast_fusion
  10.2 0.0 copy-done.1
  10.3 0.1 fusion.23
  10.3 0.0 copy-start.4
  10.3 0.1 copy.35
  10.4 0.0 copy-done
  10.4 0.5 copy-done.4
  11.0 0.2 fusion.34
  11.2 18.1 %all_gather.6 = f32[128,128]{1,0:T(8,128)S(1)} all-gather(f32[8,128]{1,0:T(8,128)S(1)} %fusion.34), channel_id=1, replica_groups=mesh['groups'=2,'space'=16] {'space'}, dimensions={0}, use_global_device_ids=true | all-gather | bytes 69632 | tf_op jit(solution)/shard_map/all_gather | solution.py:72
  29.2 0.1 copy.39
  29.3 0.3 convolution_bitcast_fusion.3
  29.6 0.0 copy-start.5
  29.6 0.0 copy-start.3
  29.6 0.1 copy.37
  29.8 0.6 copy-done.5
  30.3 0.1 div.18
  30.4 0.0 copy-start.7
  30.4 0.7 copy-done.7
  31.1 0.6 dynamic-slice.2
  32.3 0.0 copy-done.3
  32.3 0.2 fusion.33
  32.5 0.0 collective-permute-done
  32.5 0.0 collective-permute-done.1
  32.5 0.1 copy.34
  32.6 0.6 fusion.2
  33.2 1.0 convolution_bitcast_fusion.6
  34.3 1.0 convolution_bitcast_fusion.5
  35.3 0.0 all-reduce.8.cloned.1.call-update
  35.3 0.0 copy-start.6
  35.3 0.0 all-reduce.6.cloned.1.call-start
  35.4 0.6 copy-done.6
  36.0 0.2 convolution_bitcast_fusion.7
  36.2 90.3 %all-reduce.8.cloned.1.call-done = (f32[128,128]{1,0:T(8,128)}, f32[128,128]{1,0:T(8,128)}) async-done(((f32[128,128]{1,0:T(8,128)}, f32[128,128]{1,0:T(8,128)}), (f32[128,128]{1,0:T(8,128)}, f32[128,128]{1,0:T(8,128)})) %all-reduce.8.cloned.1.call-update) | async-done | bytes 131088 | tf_op jit(solution)/shard_map/psum | solution.py:48
  126.5 1.0 fusion.11
  127.4 16.9 %all_gather.7 = f32[128,128]{1,0:T(8,128)S(1)} all-gather(f32[8,128]{1,0:T(8,128)S(1)} %fusion.11), channel_id=1, replica_groups=mesh['groups'=2,'space'=16] {'space'}, dimensions={0}, use_global_device_ids=true | all-gather | bytes 69632 | tf_op jit(solution)/shard_map/all_gather | solution.py:72
  144.4 0.3 convolution_bitcast_fusion.2
  144.7 0.1 copy.42
  144.8 0.6 fusion.3
  145.4 1.0 convolution_bitcast_fusion.4
  146.4 0.0 copy-start.2
  146.4 0.0 all-reduce.6.cloned.1.call-update
  146.4 88.9 %all-reduce.6.cloned.1.call-done = f32[128,128]{1,0:T(8,128)} async-done(((f32[128,128]{1,0:T(8,128)}), f32[128,128]{1,0:T(8,128)}) %all-reduce.6.cloned.1.call-update) | async-done | bytes 65552
  235.3 0.0 copy-done.2
  235.3 1.4 fusion.7
  (5 shorter events, 0.1 us)
Async XLA Ops:
  6.5 3.9 %copy-start = (f32[256,128]{1,0:T(8,128)S(1)}, f32[256,128]{1,0:T(8,128)}, u32[]{:S(2)}) copy-start(f32[256,128]{1,0:T(8,128)} %param.9) | copy-start | bytes 393220
  6.5 3.6 %copy-start.1 = (f32[2,128,2,64]{1,3,2,0:T(8,128)S(1)}, f32[2,128,2,64]{1,3,2,0:T(8,128)}, u32[]{:S(2)}) copy-start(f32[2,128,2,64]{1,3,2,0:T(8,128)} %param.6) | copy-start | bytes 393220
  6.5 119.9 %all-reduce.8.cloned.1.call-start = ((), (), s32[]{:S(2)}) async-start(), calls=%async_computation.1 | async-start | bytes 262144 | tf_op jit(solution)/shard_map/psum | solution.py:48
  6.5 26.0 %collective-permute-start = (f32[2,128,2,64]{1,3,2,0:T(8,128)}, f32[2,128,2,64]{1,3,2,0:T(8,128)S(1)}, u32[]{:S(2)}, u32[]{:S(2)}) collective-permute-start(f32[2,128,2,64]{1,3,2,0:T(8,128)} %param.6), channel_id=1, source_target_pairs={{0,1},{1,2},{2,3},{3,4},{4,5},{5,6},{6,7},{7,8},{8,9},{9,10},{10,1... | collective-permute-start | bytes 393224 | tf_op jit(solution)/shard_map/ppermute | solution.py:18
  6.6 25.9 %collective-permute-start.1 = (f32[2,128,2,64]{1,3,2,0:T(8,128)}, f32[2,128,2,64]{1,3,2,0:T(8,128)S(1)}, u32[]{:S(2)}, u32[]{:S(2)}) collective-permute-start(f32[2,128,2,64]{1,3,2,0:T(8,128)} %param.6), channel_id=1, source_target_pairs={{1,0},{2,1},{3,2},{4,3},{5,4},{6,5},{7,6},{8,7},{9,8},{10,9},{11,1... | collective-permute-start | bytes 393224 | tf_op jit(solution)/shard_map/ppermute | solution.py:19
  10.3 0.7 copy-start.4
  29.6 0.7 copy-start.5
  29.6 2.7 %copy-start.3 = (f32[256,128]{1,0:T(8,128)S(1)}, f32[256,128]{1,0:T(8,128)}, u32[]{:S(2)}) copy-start(f32[256,128]{1,0:T(8,128)} %param.10) | copy-start | bytes 393220
  30.4 0.7 copy-start.7
  35.3 0.7 copy-start.6
  35.3 200.0 %all-reduce.6.cloned.1.call-start = ((), (), s32[]{:S(2)}) async-start(), calls=%async_computation | async-start | bytes 131072
  146.4 88.9 %copy-start.2 = (f32[128,128]{1,0:T(8,128)S(1)}, f32[128,128]{1,0:T(8,128)}, u32[]{:S(2)}) copy-start(f32[128,128]{1,0:T(8,128)} %get-tuple-element.27) | copy-start | bytes 196612
Sparse Core Ops, SparseCore 0:
  35.4 90.9 all-reduce.7
  146.5 88.7 all-reduce.5
where the time goes:
time: 244 us
  waiting for transfers between devices  179 us (73%)
  blocking collectives  35 us (14%)
  between operations  14.2 us (6%)
  matrix products  7.78 us (3%)
  local copies, waits for them, and re-layouts  4.56 us (2%)
  starting transfers between devices  2.68 us (1%)
    psum x1, waiting for transfers between devices, shards(): lax.psum(jnp.einsum('taic,tajc->ij', slopes * cell_scale[None, None, None...  90.3 us
    unnamed x3, waiting for transfers between devices  88.9 us
    all_gather x2, blocking collectives, shards(): everyone = lax.all_gather(coeffs, 'space', axis=0, tiled=True)  35 us
  transfers between devices with their start and end apart: 4, of which 2 were waited for; matrix products, arithmetic and copies ran while one was open for 1% of the time, Pallas kernels for 0%

commit v1 on v0

--- a/solution.py
+++ b/solution.py
@@ -45,14 +45,17 @@
     velocity = modes.reshape(2, mode_count, cell_count)
     cell_scale = cell_weight.reshape(cell_count) / total_cells
     weighted = velocity * cell_scale[None, None, :]
-    diffusion = lax.psum(
-        jnp.einsum(
-            "taic,tajc->ij",
-            slopes * cell_scale[None, None, None, :],
-            slopes,
-            precision=lax.Precision.HIGHEST,
+    diffusion = jnp.sum(
+        lax.all_gather(
+            jnp.einsum(
+                "taic,tajc->ij",
+                slopes * cell_scale[None, None, None, :],
+                slopes,
+                precision=lax.Precision.HIGHEST,
+            ),
+            "space",
         ),
-        "space",
+        axis=0,
     )
     selector = (
         seeds[:, None] == jnp.arange(coeff_table.shape[0], dtype=jnp.int32)[None, :]

time: 244 us -> 262 us (1.074)
  waiting for transfers between devices: 179 us -> 196 us
    unnamed x3 -> x5, waiting for transfers between devices: 88.9 us -> 180 us
    psum x1 -> x0, waiting for transfers between devices: 90.3 us -> none  [shards(): lax.psum(jnp.einsum('taic,tajc->ij', slopes * cell_scale[None, None, None...]
    all_gather x0 -> x1, waiting for transfers between devices: none -> 13.1 us  [shards(): lax.all_gather(jnp.einsum('taic,tajc->ij', slopes * cell_scale[None, None...]
    ppermute x1, waiting for transfers between devices: 0.01 us -> 2.65 us  [padded_2(): before = lax.ppermute(last, axis, up)]
  transfers between devices with their start and end apart: 4 -> 5, of which waited for: 2 -> 5; matrix products, arithmetic and copies ran while one was open for 1% -> 2% of each run, Pallas kernels for 0% -> 0%
where the time goes in v1:
time: 262 us
  waiting for transfers between devices  196 us (75%)
  blocking collectives  36.4 us (14%)
  between operations  13.9 us (5%)
  matrix products  7.58 us (3%)
  local copies, waits for them, and re-layouts  5.45 us (2%)
    unnamed x5, waiting for transfers between devices  180 us
    all_gather x2, blocking collectives, shards(): everyone = lax.all_gather(coeffs, 'space', axis=0, tiled=True)  36.4 us
    all_gather x1, waiting for transfers between devices, shards(): lax.all_gather(jnp.einsum('taic,tajc->ij', slopes * cell_scale[None, None...  13.1 us
  transfers between devices with their start and end apart: 5, of which 5 were waited for; matrix products, arithmetic and copies ran while one was open for 2% of the time, Pallas kernels for 0%

profile of v1, /device:TPU:8, one launch (start us, length us, event | category | flops | bytes accessed | tf_op | source)
XLA Modules:
  0.0 262.1 jit_solution(14714968671249141143)
XLA Ops:
  6.5 0.0 copy-start
  6.5 0.0 copy-start.1
  6.5 0.0 all-gather.3.cloned.1.call-start
  6.5 0.8 collective-permute-start.1
  7.4 0.0 collective-permute-start
  7.4 1.0 slice_bitcast_fusion
  8.4 0.0 copy-done.1
  8.4 0.0 copy-start.4
  8.4 0.7 copy-done.4
  9.1 0.1 div.18
  9.2 0.1 fusion.23
  9.2 0.1 copy.35
  9.3 0.9 collective-permute-done.1
  10.2 2.7 %collective-permute-done = f32[2,128,2,64]{1,3,2,0:T(8,128)S(1)} collective-permute-done((f32[2,128,2,64]{1,3,2,0:T(8,128)}, f32[2,128,2,64]{1,3,2,0:T(8,128)S(1)}, u32[]{:S(2)}, u32[]{:S(2)}) %collective-permute-start) | collective-permute-done | bytes 131104 | tf_op jit(solution)/shard_map/ppermute | solution.py:18
  12.9 0.1 copy.34
  13.0 1.0 convolution_bitcast_fusion.6
  14.0 0.0 all-gather.3.cloned.1.call-update
  14.0 0.0 all-reduce.5.cloned.1.call-start
  14.1 0.0 copy-start.3
  14.1 0.1 copy.39
  14.2 0.0 copy-done
  14.2 0.5 copy-done.3
  14.7 0.2 fusion.34
  14.9 19.4 %all_gather.14 = f32[128,128]{1,0:T(8,128)S(1)} all-gather(f32[8,128]{1,0:T(8,128)S(1)} %fusion.34), channel_id=1, replica_groups=mesh['groups'=2,'space'=16] {'space'}, dimensions={0}, use_global_device_ids=true | all-gather | bytes 69632 | tf_op jit(solution)/shard_map/all_gather | solution.py:75
  34.4 0.3 convolution_bitcast_fusion.3
  34.6 0.0 copy-start.2
  34.7 0.1 copy.37
  34.8 0.8 copy-done.2
  35.6 0.2 fusion.33
  35.7 0.6 fusion.2
  36.4 1.0 convolution_bitcast_fusion.5
  37.4 0.0 all-reduce.5.cloned.1.call-update
  37.4 0.0 copy-start.5
  37.4 0.0 all-reduce.7.cloned.1.call-start
  37.4 0.6 copy-done.5
  38.1 0.2 convolution_bitcast_fusion.7
  38.2 0.0 copy-start.6
  38.2 0.7 copy-done.6
  38.9 0.6 dynamic-slice.2
  40.1 13.1 %all-gather.3.cloned.1.call-done = f32[2048,128]{1,0:T(8,128)} async-done(((f32[128,128]{1,0:T(8,128)}), f32[2048,128]{1,0:T(8,128)}) %all-gather.3.cloned.1.call-update) | async-done | bytes 1048592 | tf_op jit(solution)/shard_map/all_gather | solution.py:49
  53.2 1.3 reduce_sum.29
  54.5 90.9 %all-reduce.5.cloned.1.call-done = f32[128,128]{1,0:T(8,128)} async-done(((f32[128,128]{1,0:T(8,128)}), f32[128,128]{1,0:T(8,128)}) %all-reduce.5.cloned.1.call-update) | async-done | bytes 65552
  145.5 0.8 fusion.11
  146.3 16.9 %all_gather.15 = f32[128,128]{1,0:T(8,128)S(1)} all-gather(f32[8,128]{1,0:T(8,128)S(1)} %fusion.11), channel_id=1, replica_groups=mesh['groups'=2,'space'=16] {'space'}, dimensions={0}, use_global_device_ids=true | all-gather | bytes 69632 | tf_op jit(solution)/shard_map/all_gather | solution.py:75
  163.2 0.3 convolution_bitcast_fusion.2
  163.5 0.1 copy.42
  163.6 0.6 fusion.3
  164.2 1.0 convolution_bitcast_fusion.4
  165.2 0.0 all-reduce.7.cloned.1.call-update
  165.2 88.9 %all-reduce.7.cloned.1.call-done = f32[128,128]{1,0:T(8,128)} async-done(((f32[128,128]{1,0:T(8,128)}), f32[128,128]{1,0:T(8,128)}) %all-reduce.7.cloned.1.call-update) | async-done | bytes 65552
  254.1 1.5 fusion.7
  (5 shorter events, 0.1 us)
Async XLA Ops:
  6.5 7.7 %copy-start = (f32[256,128]{1,0:T(8,128)S(1)}, f32[256,128]{1,0:T(8,128)}, u32[]{:S(2)}) copy-start(f32[256,128]{1,0:T(8,128)} %param.9) | copy-start | bytes 393220
  6.5 1.8 copy-start.1
  6.5 46.7 %all-gather.3.cloned.1.call-start = ((), (), s32[]{:S(2)}) async-start(), calls=%async_computation | async-start | bytes 1114112 | tf_op jit(solution)/shard_map/all_gather | solution.py:49
  6.5 3.7 %collective-permute-start.1 = (f32[2,128,2,64]{1,3,2,0:T(8,128)}, f32[2,128,2,64]{1,3,2,0:T(8,128)S(1)}, u32[]{:S(2)}, u32[]{:S(2)}) collective-permute-start(f32[2,128,2,64]{1,3,2,0:T(8,128)} %param.6), channel_id=1, source_target_pairs={{1,0},{2,1},{3,2},{4,3},{5,4},{6,5},{7,6},{8,7},{9,8},{10,9},{11,1... | collective-permute-start | bytes 393224 | tf_op jit(solution)/shard_map/ppermute | solution.py:19
  7.4 5.5 %collective-permute-start = (f32[2,128,2,64]{1,3,2,0:T(8,128)}, f32[2,128,2,64]{1,3,2,0:T(8,128)S(1)}, u32[]{:S(2)}, u32[]{:S(2)}) collective-permute-start(f32[2,128,2,64]{1,3,2,0:T(8,128)} %param.6), channel_id=1, source_target_pairs={{0,1},{1,2},{2,3},{3,4},{4,5},{5,6},{6,7},{7,8},{8,9},{9,10},{10,1... | collective-permute-start | bytes 393224 | tf_op jit(solution)/shard_map/ppermute | solution.py:18
  8.4 0.7 copy-start.4
  14.0 131.4 %all-reduce.5.cloned.1.call-start = ((), (), s32[]{:S(2)}) async-start(), calls=%async_computation.1 | async-start | bytes 131072
  14.1 0.7 copy-start.3
  34.6 0.9 copy-start.2
  37.4 0.7 copy-start.5
  37.4 216.7 %all-reduce.7.cloned.1.call-start = ((), (), s32[]{:S(2)}) async-start(), calls=%async_computation.2 | async-start | bytes 131072
  38.2 0.7 copy-start.6
Sparse Core Ops, SparseCore 0:
  14.1 39.0 all-gather.2
  56.7 88.7 all-reduce.4
  165.4 88.6 all-reduce.6
